TPU v7x, 32 devices: a whole 2x2x4 slice. The times are simulated.
32 devices in a mesh: grp: 2 (over y), seq: 4 (over z), head: 4 (over x, core).
Axes of the slice: x: 2, y: 2, z: 4, core: 2. Of those that a mesh axis runs over, the one named last changes fastest.
Arguments:
- token_queries: bfloat16 [4, 1024, 4096], P('grp', 'seq', 'head'), parts along dimension 0, may hold values from -6 to 6
- token_keys: bfloat16 [4, 1024, 4096], P('grp', 'seq', 'head'), parts along dimension 0, may hold values from -6 to 6
- token_values: bfloat16 [4, 1024, 4096], P('grp', 'seq', 'head'), parts along dimension 0, may hold values from -6 to 6
- step_size: float32 [8, 4, 1024], P('head', 'grp', 'seq'), parts along dimension 1, may hold values from 0.5 to 9
- fast_weights: float32 [6, 8, 512, 512], P('grp', 'head', 'seq'), parts along dimension 0, may hold values from -0.25 to 0.25
- momentum: float32 [6, 8, 512, 512], P('grp', 'head', 'seq'), parts along dimension 0, may hold values from -0.1875 to 0.1875
- fast_gain: float32 [8, 512], P('head'), may hold values from 0.5 to 1.5
Outputs:
- layer_out: bfloat16 [4, 1024, 4096], P('grp', 'seq', 'head'), parts along dimension 0
- new_weights: float32 [6, 8, 512, 512], P('grp', 'head', 'seq'), parts along dimension 0
- new_momentum: float32 [6, 8, 512, 512], P('grp', 'head', 'seq'), parts along dimension 0
There are 2 independent parts, one for each index of `grp`. A program takes and returns all parts, laid end to end along the dimension named above; an argument that names none is the same for every part. Nothing has to cross between parts.
All inputs are finite; a program needn't handle non-finite values.
Results may differ from a plain program's by a relative error of at most 0.025.
Values may be sent and summed in bfloat16 or wider, within the bound.
A program may use at most 64 MiB of HBM per device.

v0:
```python
import math

import jax
import jax.numpy as jnp
from jax import lax
from jax.sharding import PartitionSpec as P

HD = 128
WINDOW = 256


EPSILON = 1e-06
MOMENT_DECAY = 0.9
STEP_RATE = 0.02


def shifted(block, axis, distance):
    devices = range(lax.axis_size(axis))
    route = [((i - distance) % len(devices), i) for i in devices]
    return lax.ppermute(block, axis, route)


def rms_rows(values):
    return values * lax.rsqrt(jnp.mean(values * values, axis=-1, keepdims=True) + EPSILON)


def attend(query_rows, key_rows, value_rows, halo_live, head_count):
    periods, row_count, features = query_rows.shape
    key_span = key_rows.shape[1]
    query_heads = query_rows.reshape(periods, row_count, head_count, HD)
    key_heads = key_rows.reshape(periods, key_span, head_count, HD)
    value_heads = value_rows.reshape(periods, key_span, head_count, HD)
    scores = jnp.einsum(
        "pqhd,pkhd->phqk", query_heads, key_heads, preferred_element_type=jnp.float32
    )
    scores = scores * (1.0 / math.sqrt(HD))
    query_pos = lax.broadcasted_iota(jnp.int32, (row_count, key_span), 0)
    key_pos = lax.broadcasted_iota(jnp.int32, (row_count, key_span), 1) - (key_span - row_count)
    band = (key_pos <= query_pos) & (key_pos > query_pos - WINDOW)
    allowed = band[None] & ((key_pos >= 0)[None] | halo_live[:, None, None])
    scores = jnp.where(allowed[:, None], scores, -1e30)
    top = jnp.max(scores, axis=-1, keepdims=True)
    expo = jnp.exp(scores - top)
    probs = (expo / jnp.sum(expo, axis=-1, keepdims=True)).astype(jnp.bfloat16)
    mixed = jnp.einsum("phqk,pkhd->pqhd", probs, value_heads, preferred_element_type=jnp.float32)
    return mixed.reshape(periods, row_count, features)


def silu_parts(pre):
    sigma = jax.nn.sigmoid(pre)
    return (pre * sigma, sigma * (1.0 + pre * (1.0 - sigma)))


def partial_grads(casted, key_norm, targets):
    gate_pre = jnp.einsum("thi,hji->htj", key_norm, casted[0], preferred_element_type=jnp.float32)
    up_pre = jnp.einsum("thi,hji->htj", key_norm, casted[1], preferred_element_type=jnp.float32)
    active, slope = silu_parts(gate_pre)
    hidden = (active * up_pre).astype(jnp.bfloat16)
    back = -jnp.einsum("tho,hoj->htj", targets, casted[2], preferred_element_type=jnp.float32)
    d_gate = (back * up_pre * slope).astype(jnp.bfloat16)
    d_up = (back * active).astype(jnp.bfloat16)
    g_gate = jnp.einsum("htj,thi->hji", d_gate, key_norm, preferred_element_type=jnp.float32)
    g_up = jnp.einsum("htj,thi->hji", d_up, key_norm, preferred_element_type=jnp.float32)
    g_down = -jnp.einsum("tho,htj->hoj", targets, hidden, preferred_element_type=jnp.float32)
    return jnp.stack([g_gate, g_up, g_down])


def apply_fast(casted, query_norm, fast_gain):
    gate_pre = jnp.einsum("thi,hji->htj", query_norm, casted[0], preferred_element_type=jnp.float32)
    up_pre = jnp.einsum("thi,hji->htj", query_norm, casted[1], preferred_element_type=jnp.float32)
    hidden = (jax.nn.silu(gate_pre) * up_pre).astype(jnp.bfloat16)
    result = jnp.einsum("htj,hoj->tho", hidden, casted[2], preferred_element_type=jnp.float32)
    return rms_rows(result) * fast_gain[None]


def advance(weights, moment, summed, rate_total):
    moment = MOMENT_DECAY * moment + summed / rate_total[None, :, None, None]
    weights = weights - STEP_RATE * rms_rows(moment)
    return (weights, moment)


def spread_rows(weights):
    return lax.all_gather(weights.astype(jnp.bfloat16), "seq", axis=2, tiled=True)


def shards(token_queries, token_keys, token_values, step_size, fast_weights, momentum, fast_gain):
    periods, row_count, features = token_queries.shape
    head_count = features // HD
    head_width = fast_weights.shape[3]
    fast_heads = features // head_width
    seq_place = lax.axis_index("seq")
    leading = seq_place == 0
    tail_rows = shifted((token_keys, token_values), "seq", 1)
    halo_keys = jnp.where(leading, jnp.roll(tail_rows[0], 1, axis=0), tail_rows[0])
    halo_values = jnp.where(leading, jnp.roll(tail_rows[1], 1, axis=0), tail_rows[1])
    halo_live = jnp.logical_or(jnp.logical_not(leading), jnp.arange(periods, dtype=jnp.int32) > 0)
    key_all = jnp.concatenate([halo_keys, token_keys], 1)
    value_all = jnp.concatenate([halo_values, token_values], 1)
    mixed_all = attend(token_queries, key_all, value_all, halo_live, head_count)
    weight_state, moment_state = (fast_weights, momentum)
    casted = spread_rows(weight_state)
    outputs = []
    for period in range(periods):
        rates = step_size[:, period]
        key_norm = rms_rows(
            token_keys[period].reshape(row_count, fast_heads, head_width).astype(jnp.float32)
        ).astype(jnp.bfloat16)
        targets = (
            rates.T[:, :, None]
            * token_values[period].reshape(row_count, fast_heads, head_width).astype(jnp.float32)
        ).astype(jnp.bfloat16)
        partial_value = partial_grads(casted, key_norm, targets)
        rate_total = lax.psum(jnp.sum(rates, axis=1), "seq")
        summed = lax.psum_scatter(
            partial_value.astype(jnp.bfloat16), "seq", scatter_dimension=2, tiled=True
        ).astype(jnp.float32)
        weight_state, moment_state = advance(weight_state, moment_state, summed, rate_total)
        casted = spread_rows(weight_state)
        query_norm = rms_rows(
            token_queries[period].reshape(row_count, fast_heads, head_width).astype(jnp.float32)
        ).astype(jnp.bfloat16)
        fast_out = apply_fast(casted, query_norm, fast_gain).reshape(row_count, features)
        outputs.append((mixed_all[period] + fast_out).astype(jnp.bfloat16))
    return (jnp.stack(outputs), weight_state, moment_state)


def solution(mesh):
    placed = (
        P("grp", "seq", "head"),
        P("grp", "seq", "head"),
        P("grp", "seq", "head"),
        P("head", "grp", "seq"),
        P("grp", "head", "seq", None),
        P("grp", "head", "seq", None),
        P("head", None),
    )
    return jax.shard_map(
        shards,
        mesh=mesh,
        in_specs=placed,
        out_specs=(
            P("grp", "seq", "head"),
            P("grp", "head", "seq", None),
            P("grp", "head", "seq", None),
        ),
        check_vma=False,
    )
```

profile of v0, /device:TPU:9, one launch (start us, length us, event | category | flops | bytes accessed | tf_op | source)
XLA Modules:
  0.0 403.6 jit_solution(7927282134830770952)
XLA Ops:
  7.2 2.4 convert_element_type.138
  14.9 2.6 copy.190
  18.0 53.9 %all-gather.4.cloned.1.call-done = bf16[3,2,512,512]{3,2,1,0:T(8,128)(2,1)} async-done(((bf16[3,2,128,512]{3,2,1,0:T(8,128)(2,1)}), bf16[3,2,512,512]{3,2,1,0:T(8,128)(2,1)}) %all-gather.4.cloned.1.call-update) | async-done | bytes 3145744 | tf_op jit(solution)/shard_map/all_gather | solution.py:83
  78.8 2.0 pad_maximum_fusion
  80.9 9.8 %all-reduce = (f32[2]{0:T(128)S(1)}, f32[2]{0:T(128)S(1)}) all-reduce(f32[2]{0:T(128)S(1)} %get-tuple-element.4, f32[2]{0:T(128)S(1)} %get-tuple-element.3), channel_id=1, replica_groups=mesh['grp'=2,'seq'=4,'head'=4] {'seq'}, use_global_device_ids=true, to_apply=%region_5.6 | all-reduce | flops 4 | bytes 32 | tf_op jit(solution)/shard_map/psum | solution.py:113
  90.7 51.2 %reduce-scatter.3.cloned.1.call-done = bf16[3,2,128,512]{3,2,1,0:T(8,128)(2,1)} async-done(((bf16[3,2,512,512]{3,2,1,0:T(8,128)(2,1)}), bf16[3,2,128,512]{3,2,1,0:T(8,128)(2,1)}) %reduce-scatter.3.cloned.1.call-update) | async-done | bytes 786448 | tf_op jit(solution)/shard_map/reduce_scatter | solution.py:114
  141.9 2.1 multiply_reduce_fusion.1
  145.3 2.2 copy.173
  147.5 2.5 copy.191
  151.2 2.2 multiply_convert_fusion.4
  153.4 53.5 %all-gather.6.cloned.1.call-done = bf16[3,2,512,512]{3,2,1,0:T(8,128)(2,1)} async-done(((bf16[3,2,128,512]{3,2,1,0:T(8,128)(2,1)}), bf16[3,2,512,512]{3,2,1,0:T(8,128)(2,1)}) %all-gather.6.cloned.1.call-update) | async-done | bytes 3145744 | tf_op jit(solution)/shard_map/all_gather | solution.py:83
  206.9 1.9 fusion.35
  214.3 2.0 pad_maximum_fusion.1
  216.4 2.3 collective-permute-start.1
  218.7 2.3 copy.147
  221.2 2.2 fusion.56
  223.5 2.2 copy.198
  225.7 2.0 copy.199
  230.5 2.3 copy.165
  232.8 2.3 copy.179
  235.0 84.4 %reduce-scatter.5.cloned.1.call-done = bf16[3,2,128,512]{3,2,1,0:T(8,128)(2,1)} async-done(((bf16[3,2,512,512]{3,2,1,0:T(8,128)(2,1)}), bf16[3,2,128,512]{3,2,1,0:T(8,128)(2,1)}) %reduce-scatter.5.cloned.1.call-update) | async-done | bytes 786448 | tf_op jit(solution)/shard_map/reduce_scatter | solution.py:114
  321.0 1.9 fusion.54
  325.5 1.9 maximum_select_fusion
  330.3 3.8 fusion.60
  336.4 2.7 copy.180
  339.1 2.5 copy.166
  341.6 2.7 fusion.34
  344.3 3.5 multiply_reduce_fusion.5
  347.8 35.1 %all-gather.8.cloned.1.call-done = bf16[3,2,512,512]{3,2,1,0:T(8,128)(2,1)} async-done(((bf16[3,2,128,512]{3,2,1,0:T(8,128)(2,1)}), bf16[3,2,512,512]{3,2,1,0:T(8,128)(2,1)}) %all-gather.8.cloned.1.call-update) | async-done | bytes 3145744 | tf_op jit(solution)/shard_map/all_gather | solution.py:83
  382.9 3.0 fusion.18
  385.9 2.9 multiply_reduce_fusion.2
  392.1 2.6 copy.167
  (102 shorter events, 38.6 us)
Async XLA Ops:
  7.2 64.7 %all-gather.4.cloned.1.call-start = ((), (), s32[]{:S(2)}) async-start(), calls=%async_computation.2 | async-start | bytes 3932160 | tf_op jit(solution)/shard_map/all_gather | solution.py:83
  9.6 3.8 copy-start.6
  9.6 132.3 %reduce-scatter.3.cloned.1.call-start = ((), (), s32[]{:S(2)}) async-start(), calls=%async_computation.3 | async-start | bytes 3932160 | tf_op jit(solution)/shard_map/reduce_scatter | solution.py:114
  11.2 3.7 copy-start.1
  12.2 5.4 %copy-start.17 = (f32[2,2,256]{2,1,0:T(2,128)S(1)}, f32[2,2,256]{2,1,0:T(2,128)}, u32[]{:S(2)}) copy-start(f32[2,2,256]{2,1,0:T(2,128)} %param.10) | copy-start | bytes 12292
  14.9 2.9 copy-start.7
  17.8 57.4 %copy-start.13 = (f32[1,256,1024]{1,2,0:T(8,128)S(1)}, f32[1,256,1024]{1,2,0:T(8,128)}, u32[]{:S(2)}) copy-start(f32[1,256,1024]{1,2,0:T(8,128)} %copy.190) | copy-start | bytes 3145732
  80.8 63.2 %copy-start = (f32[3,2,128,512]{3,2,1,0:T(8,128)S(1)}, f32[3,2,128,512]{3,2,1,0:T(8,128)}, u32[]{:S(2)}) copy-start(f32[3,2,128,512]{3,2,1,0:T(8,128)} %param.11) | copy-start | bytes 4718596
  80.9 126.0 %all-gather.6.cloned.1.call-start = ((), (), s32[]{:S(2)}) async-start(), calls=%async_computation.4 | async-start | bytes 3932160 | tf_op jit(solution)/shard_map/all_gather | solution.py:83
  145.2 174.2 %reduce-scatter.5.cloned.1.call-start = ((), (), s32[]{:S(2)}) async-start(), calls=%async_computation.5 | async-start | bytes 3932160 | tf_op jit(solution)/shard_map/reduce_scatter | solution.py:114
  206.9 3.8 copy-start.14
  210.7 2.3 copy-start.5
  216.4 166.5 %all-gather.8.cloned.1.call-start = ((), (), s32[]{:S(2)}) async-start(), calls=%async_computation.6 | async-start | bytes 3932160 | tf_op jit(solution)/shard_map/all_gather | solution.py:83
  216.4 107.8 %collective-permute-start.1 = (bf16[2,256,1024]{1,2,0:T(8,128)(2,1)}, bf16[2,256,1024]{1,2,0:T(8,128)(2,1)}, u32[]{:S(2)}, u32[]{:S(2)}) collective-permute-start(bf16[2,256,1024]{1,2,0:T(8,128)(2,1)} %copy-done.1), channel_id=1, source_target_pairs={{12,0},{0,4},{4,8},{8,12},{13,1},{1,5},{5,9},{9,13},{14,2},{2,6},{... | collective-permute-start | bytes 3145736 | tf_op jit(solution)/shard_map/ppermute | solution.py:20
  220.9 102.0 %collective-permute-start = (bf16[2,256,1024]{1,2,0:T(8,128)(2,1)}, bf16[2,256,1024]{1,2,0:T(8,128)(2,1)}, u32[]{:S(2)}, u32[]{:S(2)}) collective-permute-start(bf16[2,256,1024]{1,2,0:T(8,128)(2,1)} %copy.147), channel_id=1, source_target_pairs={{12,0},{0,4},{4,8},{8,12},{13,1},{1,5},{5,9},{9,13},{14,2},{2,6},{... | collective-permute-start | bytes 3145736 | tf_op jit(solution)/shard_map/ppermute | solution.py:20
  321.0 1.9 copy-start.3
  325.5 1.9 copy-start.11
  327.4 1.2 copy-start.2
  327.6 1.4 copy-start.15
  336.4 5.3 %copy-start.4 = (bf16[3,2,512,512]{3,2,1,0:T(8,128)(2,1)S(1)}, bf16[3,2,512,512]{3,2,1,0:T(8,128)(2,1)}, u32[]{:S(2)}) copy-start(bf16[3,2,512,512]{3,2,1,0:T(8,128)(2,1)} %all-gather.6.cloned.1.call-done) | copy-start | bytes 9437188
  347.8 38.1 %copy-start.12 = (f32[256,2,512]{2,0,1:T(8,128)S(1)}, f32[256,2,512]{2,0,1:T(8,128)}, u32[]{:S(2)}) copy-start(f32[256,2,512]{2,0,1:T(8,128)} %copy.179) | copy-start | bytes 3145732
  385.9 2.9 copy-start.16
  385.9 2.9 copy-start.18
  390.4 4.3 %copy-start.8 = (f32[1,256,1024]{2,1,0:T(8,128)S(1)}, f32[1,256,1024]{2,1,0:T(8,128)}, u32[]{:S(2)}) copy-start(f32[1,256,1024]{2,1,0:T(8,128)} %copy.180) | copy-start | bytes 3145732
  390.4 4.5 %copy-start.9 = (f32[1,256,1024]{2,1,0:T(8,128)S(1)}, f32[1,256,1024]{2,1,0:T(8,128)}, u32[]{:S(2)}) copy-start(f32[1,256,1024]{2,1,0:T(8,128)} %copy.166) | copy-start | bytes 3145732
  394.7 1.2 copy-start.10
Sparse Core Ops, SparseCore 0:
  9.8 62.0 all-gather.3
  81.0 60.9 reduce-scatter.2
  145.3 61.5 all-gather.5
  216.5 102.8 reduce-scatter.4
  323.1 59.7 all-gather.7
where the time goes:
time: 409 us; the launch traced here: 404 us
  waiting for transfers between devices  278 us (68%)
  local copies, waits for them, and re-layouts  40.2 us (10%)
  other arithmetic  30.2 us (7%)
  matrix products  28.3 us (7%)
  between operations  14.2 us (3%)
  blocking collectives  9.79 us (2%)
    all_gather x3, waiting for transfers between devices, spread_rows(): lax.all_gather(weights.astype(jnp.bfloat16), 'seq', axis=2, tiled=True)  143 us
    reduce_scatter x2, waiting for transfers between devices, shards(): lax.psum_scatter(partial_value.astype(jnp.bfloat16), 'seq', scatter_dimen...  136 us
    unnamed x44, local copies, waits for them, and re-layouts  10.4 us
    psum x1, blocking collectives, shards(): rate_total = lax.psum(jnp.sum(rates, axis=1), 'seq')  9.79 us
  transfers between devices with their start and end apart: 7, of which 5 were waited for; matrix products, arithmetic and copies ran while one was open for 15% of the time, Pallas kernels for 0%

commit v1 on v0

--- a/solution.py
+++ b/solution.py
@@ -1,8 +1,11 @@
+import functools
 import math
 
 import jax
 import jax.numpy as jnp
 from jax import lax
+from jax.experimental import pallas as pl
+from jax.experimental.pallas import tpu as pltpu
 from jax.sharding import PartitionSpec as P
 
 HD = 128
@@ -83,7 +86,7 @@
     return lax.all_gather(weights.astype(jnp.bfloat16), "seq", axis=2, tiled=True)
 
 
-def shards(token_queries, token_keys, token_values, step_size, fast_weights, momentum, fast_gain):
+def split_shards(token_queries, token_keys, token_values, step_size, fast_weights, momentum, fast_gain):
     periods, row_count, features = token_queries.shape
     head_count = features // HD
     head_width = fast_weights.shape[3]
@@ -124,6 +127,375 @@
     return (jnp.stack(outputs), weight_state, moment_state)
 
 
+def dot_rows(x, y):
+    return lax.dot_general(x, y, (((1,), (1,)), ((), ())), preferred_element_type=jnp.float32)
+
+
+def dot_tokens(x, y):
+    return lax.dot_general(x, y, (((0,), (0,)), ((), ())), preferred_element_type=jnp.float32)
+
+
+def dot_plain(x, y):
+    return lax.dot_general(x, y, (((1,), (0,)), ((), ())), preferred_element_type=jnp.float32)
+
+
+def hub_kernel(
+    n,
+    periods,
+    q_ref,
+    k_ref,
+    v_ref,
+    r_ref,
+    wb_ref,
+    mb_ref,
+    w_ref,
+    m_ref,
+    gain_ref,
+    layer_ref,
+    nw_ref,
+    nm_ref,
+    qb,
+    kb,
+    vb,
+    rb,
+    wblk,
+    mblk,
+    wf,
+    mf,
+    gacc,
+    gs,
+    gin,
+    lbuf,
+    fast,
+    in_send,
+    in_recv,
+    g_send,
+    g_recv,
+    l_send,
+    l_recv,
+):
+    half = n // 2
+    me = lax.axis_index("seq")
+    rows, width = kb.shape[1], kb.shape[2]
+    share = width // n
+    left = me < half
+    near_h = jnp.where(left, 0, 1)
+    far_h = 1 - near_h
+    near_hub = half - 1 + near_h
+    far_hub = half - 1 + far_h
+    is_hub = me == near_hub
+    mesh_id = pl.DeviceIdType.MESH
+
+    barrier = pltpu.get_barrier_semaphore()
+    for z in range(n):
+
+        @pl.when(me != z)
+        def _():
+            pl.semaphore_signal(barrier, inc=1, device_id={"seq": z}, device_id_type=mesh_id)
+
+    pl.semaphore_wait(barrier, n - 1)
+
+    def columns(h):
+        return pl.ds(pl.multiple_of(h * width, width), width)
+
+    def own_rows(z):
+        return pl.ds(pl.multiple_of(z * share, share), share)
+
+    inward = [
+        (lambda h: wb_ref.at[:, h], lambda z: wblk.at[:, own_rows(z)]),
+        (lambda h: r_ref.at[h], lambda z: rb.at[z]),
+    ]
+
+    def tokens(ref, buf, p):
+        return (lambda h: ref.at[p, :, columns(h)], lambda z: buf.at[p * n + z])
+
+    kind = {"w": 0, "r": 1}
+    for p in range(periods):
+        kind["k", p] = len(inward)
+        inward.append(tokens(k_ref, kb, p))
+        kind["v", p] = len(inward)
+        inward.append(tokens(v_ref, vb, p))
+        if p == 0:
+            kind["m"] = len(inward)
+            inward.append((lambda h: mb_ref.at[:, h], lambda z: mblk.at[:, own_rows(z)]))
+        kind["q", p] = len(inward)
+        inward.append(tokens(q_ref, qb, p))
+
+    def in_remote(i, h, hub, which, z):
+        src, dst = inward[i]
+        return pltpu.make_async_remote_copy(
+            src_ref=src(h),
+            dst_ref=dst(z),
+            send_sem=in_send.at[i, which],
+            recv_sem=in_recv.at[i, z],
+            device_id={"seq": hub},
+            device_id_type=mesh_id,
+        )
+
+    def in_local(i):
+        src, dst = inward[i]
+        return pltpu.make_async_copy(src(near_h), dst(me), in_recv.at[i, me])
+
+    for i in range(len(inward)):
+        in_remote(i, far_h, far_hub, 1, me).start()
+
+        @pl.when(is_hub)
+        def _():
+            in_local(i).start()
+
+        @pl.when(jnp.logical_not(is_hub))
+        def _():
+            in_remote(i, near_h, near_hub, 0, me).start()
+
+    def await_in(i):
+        for z in range(n):
+
+            @pl.when(me == z)
+            def _():
+                in_local(i).wait()
+
+            @pl.when(me != z)
+            def _():
+                in_remote(i, near_h, far_hub, 0, z).wait_recv()
+
+    def out_remote(what, p, z, h):
+        if what == "g":
+            src, dst, ss, rs = gs.at[p, z], gin.at[p, h], g_send, g_recv
+        else:
+            src, dst = lbuf.at[p * n + z], layer_ref.at[p, :, columns(h)]
+            ss, rs = l_send, l_recv
+        return pltpu.make_async_remote_copy(
+            src_ref=src,
+            dst_ref=dst,
+            send_sem=ss.at[p, z],
+            recv_sem=rs.at[p, h],
+            device_id={"seq": z},
+            device_id_type=mesh_id,
+        )
+
+    def out_local(what, p):
+        if what == "g":
+            return pltpu.make_async_copy(gs.at[p, me], gin.at[p, near_h], g_recv.at[p, near_h])
+        return pltpu.make_async_copy(
+            lbuf.at[p * n + me], layer_ref.at[p, :, columns(near_h)], l_recv.at[p, near_h]
+        )
+
+    def send_out(what, p):
+        for z in range(n):
+
+            @pl.when(me == z)
+            def _():
+                out_local(what, p).start()
+
+            @pl.when(me != z)
+            def _():
+                out_remote(what, p, z, near_h).start()
+
+    def await_out(what, p):
+        for h in range(2):
+
+            @pl.when(me == half - 1 + h)
+            def _():
+                out_local(what, p).wait()
+
+            @pl.when(me != half - 1 + h)
+            def _():
+                out_remote(what, p, half - 1 + h, h).wait_recv()
+
+    def rate_total(p):
+        total = jnp.sum(rb[0, p : p + 1, :], axis=1, keepdims=True)
+        for z in range(1, n):
+            total = total + jnp.sum(rb[z, p : p + 1, :], axis=1, keepdims=True)
+        return total
+
+    @pl.when(is_hub)
+    def _():
+        gain = gain_ref[pl.ds(near_h, 1), :]
+        row_pos = lax.broadcasted_iota(jnp.int32, (rows, rows), 0)
+        col_pos = lax.broadcasted_iota(jnp.int32, (rows, rows), 1)
+        causal = col_pos <= row_pos
+        await_in(kind["w"])
+        await_in(kind["r"])
+        for p in range(periods):
+            await_in(kind["k", p])
+            await_in(kind["v", p])
+            gacc[...] = jnp.zeros_like(gacc)
+
+            def grad_step(z, carry):
+                key_norm = rms_rows(kb[p * n + z].astype(jnp.float32)).astype(jnp.bfloat16)
+                gate_pre = dot_rows(key_norm, wblk[0])
+                up_pre = dot_rows(key_norm, wblk[1])
+                rates = jnp.broadcast_to(rb[z, p : p + 1, :], (HD, rows)).T[:, :1]
+                targets = (rates * vb[p * n + z].astype(jnp.float32)).astype(jnp.bfloat16)
+                back = -dot_plain(targets, wblk[2])
+                active, slope = silu_parts(gate_pre)
+                hidden = (active * up_pre).astype(jnp.bfloat16)
+                d_gate = (back * up_pre * slope).astype(jnp.bfloat16)
+                d_up = (back * active).astype(jnp.bfloat16)
+                gacc[0] += dot_tokens(d_gate, key_norm)
+                gacc[1] += dot_tokens(d_up, key_norm)
+                gacc[2] -= dot_tokens(targets, hidden)
+                return carry
+
+            lax.fori_loop(0, n, grad_step, 0)
+            if p == 0:
+                await_in(kind["m"])
+            total = rate_total(p)
+
+            def update_step(z, carry):
+                part = own_rows(z)
+                for i in range(3):
+                    step = gacc[i, part, :] / total
+                    gs[p, z, i] = step.astype(jnp.bfloat16)
+                    old_m = mblk[i, part, :].astype(jnp.float32) if p == 0 else mf[i, part, :]
+                    old_w = wblk[i, part, :].astype(jnp.float32) if p == 0 else wf[i, part, :]
+                    moment = MOMENT_DECAY * old_m + step
+                    weight = old_w - STEP_RATE * rms_rows(moment)
+                    mf[i, part, :] = moment
+                    wf[i, part, :] = weight
+                    wblk[i, part, :] = weight.astype(jnp.bfloat16)
+                return carry
+
+            lax.fori_loop(0, n, update_step, 0)
+            await_in(kind["q", p])
+            send_out("g", p)
+
+            def apply_step(z, carry):
+                g = p * n + z
+                query_norm = rms_rows(qb[g].astype(jnp.float32)).astype(jnp.bfloat16)
+                gate_pre = dot_rows(query_norm, wblk[0])
+                up_pre = dot_rows(query_norm, wblk[1])
+                hidden = (jax.nn.silu(gate_pre) * up_pre).astype(jnp.bfloat16)
+                fast[...] = rms_rows(dot_rows(hidden, wblk[2])) * gain
+                before = jnp.maximum(g - 1, 0)
+                for head in range(width // HD):
+                    cut = slice(head * HD, (head + 1) * HD)
+                    query = qb[g, :, cut]
+                    here = dot_rows(query, kb[g, :, cut])
+                    past = dot_rows(query, kb[before, :, cut])
+                    past = jnp.where(g > 0, past, -1e30 * math.sqrt(HD))
+                    scores = jnp.where(causal, here, past) * (1.0 / math.sqrt(HD))
+                    top = jnp.max(scores, axis=-1, keepdims=True)
+                    expo = jnp.exp(scores - top)
+                    probs = expo / jnp.sum(expo, axis=-1, keepdims=True)
+                    own = jnp.where(causal, probs, 0.0).astype(jnp.bfloat16)
+                    old = jnp.where(causal, 0.0, probs).astype(jnp.bfloat16)
+                    mixed = dot_plain(own, vb[g, :, cut]) + dot_plain(old, vb[before, :, cut])
+                    lbuf[g, :, cut] = (mixed + fast[:, cut]).astype(jnp.bfloat16)
+                return carry
+
+            lax.fori_loop(0, n, apply_step, 0)
+            send_out("l", p)
+
+    def own_step(h):
+        for i in range(3):
+            moment = m_ref[i, h]
+            weight = w_ref[i, h]
+            for p in range(periods):
+                moment = MOMENT_DECAY * moment + gin[p, h, i].astype(jnp.float32)
+                weight = weight - STEP_RATE * rms_rows(moment)
+            nm_ref[i, h] = moment
+            nw_ref[i, h] = weight
+
+    for p in range(periods):
+        await_out("g", p)
+    for h in range(2):
+        own_step(h)
+    for p in range(periods):
+        await_out("l", p)
+
+    @pl.when(is_hub)
+    def _():
+        for p in range(periods):
+            for z in range(n):
+
+                @pl.when(me != z)
+                def _():
+                    out_remote("g", p, z, near_h).wait_send()
+                    out_remote("l", p, z, near_h).wait_send()
+
+    for i in range(len(inward)):
+        in_remote(i, far_h, far_hub, 1, me).wait_send()
+
+        @pl.when(jnp.logical_not(is_hub))
+        def _():
+            in_remote(i, near_h, near_hub, 0, me).wait_send()
+
+
+def hub_shards(
+    token_queries, token_keys, token_values, step_size, fast_weights, momentum, fast_gain
+):
+    periods, rows, features = token_queries.shape
+    parts, heads, share, width = fast_weights.shape
+    n = lax.axis_size("seq")
+    bf16, f32 = jnp.bfloat16, jnp.float32
+    kinds = 3 + 3 * periods
+    vmem = pl.BlockSpec(memory_space=pltpu.VMEM)
+    anywhere = pl.BlockSpec(memory_space=pl.ANY)
+    square = (parts, width, width)
+    stream = pltpu.VMEM((periods * n, rows, width), bf16)
+    dma = pltpu.SemaphoreType.DMA
+    return pl.pallas_call(
+        functools.partial(hub_kernel, n, periods),
+        out_shape=(
+            jax.ShapeDtypeStruct(token_queries.shape, bf16),
+            jax.ShapeDtypeStruct(fast_weights.shape, f32),
+            jax.ShapeDtypeStruct(momentum.shape, f32),
+        ),
+        in_specs=[anywhere] * 6 + [vmem] * 3,
+        out_specs=(anywhere, vmem, vmem),
+        scratch_shapes=[
+            stream,
+            stream,
+            stream,
+            pltpu.VMEM((n, periods, rows), f32),
+            pltpu.VMEM(square, bf16),
+            pltpu.VMEM(square, bf16),
+            pltpu.VMEM(square, f32),
+            pltpu.VMEM(square, f32),
+            pltpu.VMEM(square, f32),
+            pltpu.VMEM((periods, n, parts, share, width), bf16),
+            pltpu.VMEM((periods, heads, parts, share, width), bf16),
+            stream,
+            pltpu.VMEM((rows, width), f32),
+            dma((kinds, 2)),
+            dma((kinds, n)),
+            dma((periods, n)),
+            dma((periods, heads)),
+            dma((periods, n)),
+            dma((periods, heads)),
+        ],
+        compiler_params=pltpu.CompilerParams(
+            collective_id=0, has_side_effects=True, vmem_limit_bytes=56 * 1024 * 1024
+        ),
+    )(
+        token_queries,
+        token_keys,
+        token_values,
+        step_size,
+        fast_weights.astype(bf16),
+        momentum.astype(bf16),
+        fast_weights,
+        momentum,
+        fast_gain,
+    )
+
+
+def shards(token_queries, token_keys, token_values, step_size, fast_weights, momentum, fast_gain):
+    args = (
+        token_queries,
+        token_keys,
+        token_values,
+        step_size,
+        fast_weights,
+        momentum,
+        fast_gain,
+    )
+    n = lax.axis_size("seq")
+    two_hubs = fast_weights.shape[1] == 2 and n % 2 == 0 and token_queries.shape[1] == WINDOW
+    return hub_shards(*args) if two_hubs else split_shards(*args)
+
+
 def solution(mesh):
     placed = (
         P("grp", "seq", "head"),

time: 409 us -> 176 us (0.43); the launches traced: 404 us -> 175 us
  waiting for transfers between devices: 278 us -> 0 us
  Pallas kernels: 0 us -> 166 us
  local copies, waits for them, and re-layouts: 40.2 us -> 5.51 us
  matrix products: 28.3 us -> 0 us
  other arithmetic: 30.2 us -> 3.49 us
  between operations: 14.2 us -> 0.66 us
  blocking collectives: 9.79 us -> 0 us
    pallas_call x0 -> x1, Pallas kernels: none -> 166 us  [hub_shards(): pl.pallas_call(functools.partial(hub_kernel, n, periods), out_shape=(jax....]
    all_gather x3 -> x0, waiting for transfers between devices: 143 us -> none  [spread_rows(): lax.all_gather(weights.astype(jnp.bfloat16), 'seq', axis=2, tiled=True)]
    reduce_scatter x2 -> x0, waiting for transfers between devices: 136 us -> none  [shards(): lax.psum_scatter(partial_value.astype(jnp.bfloat16), 'seq', scatter_dimen...]
    dot_general x18 -> x0, matrix products: 28.3 us -> none  [the longest x2 6.33 us: apply_fast(): jnp.einsum('htj,hoj->tho', hidden, casted[2], preferred_element_type=jnp....]
    convert_element_type x6 -> x0, local copies, waits for them, and re-layouts: 13.1 us -> none  [the longest x2 5.17 us: shards(): token_values[period].reshape(row_count, fast_heads, head_width)]
    psum x1 -> x0, blocking collectives: 9.79 us -> none  [shards(): rate_total = lax.psum(jnp.sum(rates, axis=1), 'seq')]
    reduce_sum x7 -> x0, other arithmetic: 7.41 us -> none  [the longest x6 7.3 us: rms_rows(): jnp.mean(values * values, axis=-1, keepdims=True) + EPSILON]
    slice x5 -> x0, local copies, waits for them, and re-layouts: 7.16 us -> none  [the longest x1 2.23 us: shards(): token_queries[period].reshape(row_count, fast_heads, head_width)]
  transfers between devices with their start and end apart: 7 -> 0, of which waited for: 5 -> 0; matrix products, arithmetic and copies ran while one was open for 15% -> 0% of each run, Pallas kernels for 0% -> 0%
where the time goes in v1:
time: 176 us; the launch traced here: 175 us
  Pallas kernels  166 us (94%)
  local copies, waits for them, and re-layouts  5.51 us (3%)
  other arithmetic  3.49 us (2%)
    pallas_call x1, Pallas kernels, hub_shards(): pl.pallas_call(functools.partial(hub_kernel, n, periods), out_shape=(jax....  166 us
    unnamed x9, local copies, waits for them, and re-layouts  5.51 us

profile of v1, /device:TPU:9, one launch (start us, length us, event | category | flops | bytes accessed | tf_op | source)
XLA Modules:
  0.0 175.3 jit_solution(9343791275904637279)
XLA Ops:
  0.6 0.0 copy-start
  0.6 2.5 %convert_element_type.6.wb_ref = bf16[3,2,128,512]{3,2,1,0:T(8,128)(2,1)} convert(f32[3,2,128,512]{3,2,1,0:T(8,128)} %w_ref.1) | non-fusion elementwise | flops 393216 | bytes 2359296 | tf_op jit(solution)/shard_map/convert_element_type | solution.py:476
  3.1 0.0 copy-done
  3.1 1.0 convert_element_type.7.mb_ref
  4.1 165.7 %shard_map.94 = (bf16[2,256,1024]{2,1,0:T(8,128)(2,1)}, f32[3,2,128,512]{3,2,1,0:T(8,128)}, f32[3,2,128,512]{3,2,1,0:T(8,128)}) custom-call(bf16[2,256,1024]{2,1,0:T(8,128)(2,1)} %q_ref.1, bf16[2,256,1024]{2,1,0:T(8,128)(2,1)} %k_ref.1, bf16[2,256,1024]{2,1,0:T(8,128)(2,1)} %v_ref.1, f32[2,2,256]{2,1,0:T(2,128)} %r_ref.1, ...), custom_call_target="tpu_custom_call" | custom-call | tf_op jit(solution)/shard_map/pallas_call | solution.py:438
  169.8 0.0 copy-start.2
  169.8 2.4 %copy.13 = bf16[2,256,1024]{2,1,0:T(8,128)(2,1)} copy(bf16[2,256,1024]{2,1,0:T(8,128)(2,1)} %get-tuple-element.6) | data formatting | bytes 2097152
  172.2 0.0 copy-done.2
  172.2 0.0 copy-start.1
  172.2 1.1 copy.14
  173.3 0.8 copy-done.1
  174.2 1.1 copy.15
Async XLA Ops:
  0.6 2.5 %copy-start = (f32[3,2,128,512]{3,2,1,0:T(8,128)S(1)}, f32[3,2,128,512]{3,2,1,0:T(8,128)}, u32[]{:S(2)}) copy-start(f32[3,2,128,512]{3,2,1,0:T(8,128)} %m_ref.1) | copy-start | bytes 4718596
  169.8 2.4 %copy-start.2 = (f32[3,2,128,512]{3,2,1,0:T(8,128)S(1)}, f32[3,2,128,512]{3,2,1,0:T(8,128)}, u32[]{:S(2)}) copy-start(f32[3,2,128,512]{3,2,1,0:T(8,128)} %get-tuple-element.7) | copy-start | bytes 4718596
  172.2 2.0 %copy-start.1 = (f32[3,2,128,512]{3,2,1,0:T(8,128)S(1)}, f32[3,2,128,512]{3,2,1,0:T(8,128)}, u32[]{:S(2)}) copy-start(f32[3,2,128,512]{3,2,1,0:T(8,128)} %get-tuple-element.8) | copy-start | bytes 4718596

commit v2 on v1

--- a/solution.py
+++ b/solution.py
@@ -146,14 +146,14 @@
     k_ref,
     v_ref,
     r_ref,
-    wb_ref,
-    mb_ref,
     w_ref,
     m_ref,
     gain_ref,
     layer_ref,
     nw_ref,
     nm_ref,
+    wb_ref,
+    mb_ref,
     qb,
     kb,
     vb,
@@ -201,21 +201,22 @@
     def own_rows(z):
         return pl.ds(pl.multiple_of(z * share, share), share)
 
-    inward = [
-        (lambda h: wb_ref.at[:, h], lambda z: wblk.at[:, own_rows(z)]),
-        (lambda h: r_ref.at[h], lambda z: rb.at[z]),
-    ]
+    inward = []
 
     def tokens(ref, buf, p):
         return (lambda h: ref.at[p, :, columns(h)], lambda z: buf.at[p * n + z])
 
-    kind = {"w": 0, "r": 1}
+    kind = {}
     for p in range(periods):
         kind["k", p] = len(inward)
         inward.append(tokens(k_ref, kb, p))
         kind["v", p] = len(inward)
         inward.append(tokens(v_ref, vb, p))
         if p == 0:
+            kind["w"] = len(inward)
+            inward.append((lambda h: wb_ref.at[:, h], lambda z: wblk.at[:, own_rows(z)]))
+            kind["r"] = len(inward)
+            inward.append((lambda h: r_ref.at[h], lambda z: rb.at[z]))
             kind["m"] = len(inward)
             inward.append((lambda h: mb_ref.at[:, h], lambda z: mblk.at[:, own_rows(z)]))
         kind["q", p] = len(inward)
@@ -237,6 +238,9 @@
         return pltpu.make_async_copy(src(near_h), dst(me), in_recv.at[i, me])
 
     for i in range(len(inward)):
+        if i == kind["w"]:
+            wb_ref[...] = w_ref[...].astype(jnp.bfloat16)
+            mb_ref[...] = m_ref[...].astype(jnp.bfloat16)
         in_remote(i, far_h, far_hub, 1, me).start()
 
         @pl.when(is_hub)
@@ -319,6 +323,9 @@
         for p in range(periods):
             await_in(kind["k", p])
             await_in(kind["v", p])
+            if p > 0:
+                send_out("g", p - 1)
+                send_out("l", p - 1)
             gacc[...] = jnp.zeros_like(gacc)
 
             def grad_step(z, carry):
@@ -357,8 +364,9 @@
                 return carry
 
             lax.fori_loop(0, n, update_step, 0)
+            if p == periods - 1:
+                send_out("g", p)
             await_in(kind["q", p])
-            send_out("g", p)
 
             def apply_step(z, carry):
                 g = p * n + z
@@ -385,7 +393,8 @@
                 return carry
 
             lax.fori_loop(0, n, apply_step, 0)
-            send_out("l", p)
+            if p == periods - 1:
+                send_out("l", p)
 
     def own_step(h):
         for i in range(3):
@@ -442,9 +451,11 @@
             jax.ShapeDtypeStruct(fast_weights.shape, f32),
             jax.ShapeDtypeStruct(momentum.shape, f32),
         ),
-        in_specs=[anywhere] * 6 + [vmem] * 3,
-        out_specs=(anywhere, vmem, vmem),
+        in_specs=[anywhere] * 4 + [vmem] * 3,
+        out_specs=(vmem, vmem, vmem),
         scratch_shapes=[
+            pltpu.VMEM(fast_weights.shape, bf16),
+            pltpu.VMEM(momentum.shape, bf16),
             stream,
             stream,
             stream,
@@ -473,8 +484,6 @@
         token_keys,
         token_values,
         step_size,
-        fast_weights.astype(bf16),
-        momentum.astype(bf16),
         fast_weights,
         momentum,
         fast_gain,

time: 176 us -> 172 us (0.977)
  other arithmetic: 3.49 us -> 0 us
    convert_element_type x2 -> x0, other arithmetic: 3.49 us -> none  [the longest x1 2.51 us: hub_shards(): fast_weights.astype(bf16)]
    unnamed x9 -> x7, local copies, waits for them, and re-layouts: 5.51 us -> 5.5 us
where the time goes in v2:
time: 172 us
  Pallas kernels  166 us (97%)
  local copies, waits for them, and re-layouts  5.5 us (3%)
    pallas_call x1, Pallas kernels, hub_shards(): pl.pallas_call(functools.partial(hub_kernel, n, periods), out_shape=(jax....  166 us
    unnamed x7, local copies, waits for them, and re-layouts  5.5 us

profile of v2, /device:TPU:9, one launch (start us, length us, event | category | flops | bytes accessed | tf_op | source)
XLA Modules:
  0.0 172.1 jit_solution(10618070332550008676)
XLA Ops:
  0.6 165.9 %shard_map.94 = (bf16[2,256,1024]{2,1,0:T(8,128)(2,1)}, f32[3,2,128,512]{3,2,1,0:T(8,128)}, f32[3,2,128,512]{3,2,1,0:T(8,128)}) custom-call(bf16[2,256,1024]{2,1,0:T(8,128)(2,1)} %q_ref.1, bf16[2,256,1024]{2,1,0:T(8,128)(2,1)} %k_ref.1, bf16[2,256,1024]{2,1,0:T(8,128)(2,1)} %v_ref.1, f32[2,2,256]{2,1,0:T(2,128)} %r_ref.1, f32[3,2,128,512]{3,2,1,0:T(8,128)} %w_ref.1, ...), custom_call_target="tpu_custom_call" | custom-call | tf_op jit(solution)/shard_map/pallas_call | solution.py:447
  166.6 0.0 copy-start.1
  166.6 2.4 %copy.13 = bf16[2,256,1024]{2,1,0:T(8,128)(2,1)} copy(bf16[2,256,1024]{2,1,0:T(8,128)(2,1)} %get-tuple-element.6) | data formatting | bytes 2097152
  169.0 0.0 copy-done.1
  169.0 0.0 copy-start
  169.0 1.1 copy.14
  170.1 0.8 copy-done
  170.9 1.1 copy.15
Async XLA Ops:
  166.6 2.4 %copy-start.1 = (f32[3,2,128,512]{3,2,1,0:T(8,128)S(1)}, f32[3,2,128,512]{3,2,1,0:T(8,128)}, u32[]{:S(2)}) copy-start(f32[3,2,128,512]{3,2,1,0:T(8,128)} %get-tuple-element.7) | copy-start | bytes 4718596
  169.0 2.0 %copy-start = (f32[3,2,128,512]{3,2,1,0:T(8,128)S(1)}, f32[3,2,128,512]{3,2,1,0:T(8,128)}, u32[]{:S(2)}) copy-start(f32[3,2,128,512]{3,2,1,0:T(8,128)} %get-tuple-element.8) | copy-start | bytes 4718596

commit v3 on v2

--- a/solution.py
+++ b/solution.py
@@ -241,15 +241,20 @@
         if i == kind["w"]:
             wb_ref[...] = w_ref[...].astype(jnp.bfloat16)
             mb_ref[...] = m_ref[...].astype(jnp.bfloat16)
-        in_remote(i, far_h, far_hub, 1, me).start()
 
         @pl.when(is_hub)
         def _():
             in_local(i).start()
+            in_remote(i, far_h, far_hub, 1, me).start()
 
         @pl.when(jnp.logical_not(is_hub))
         def _():
             in_remote(i, near_h, near_hub, 0, me).start()
+
+    @pl.when(jnp.logical_not(is_hub))
+    def _():
+        for i in range(len(inward)):
+            in_remote(i, far_h, far_hub, 1, me).start()
 
     def await_in(i):
         for z in range(n):
@@ -284,14 +289,20 @@
             lbuf.at[p * n + me], layer_ref.at[p, :, columns(near_h)], l_recv.at[p, near_h]
         )
 
-    def send_out(what, p):
+    def send_near(what, p):
+        out_local(what, p).start()
         for z in range(n):
-
-            @pl.when(me == z)
+            same_side = left if z < half else jnp.logical_not(left)
+
+            @pl.when(jnp.logical_and(same_side, me != z))
             def _():
-                out_local(what, p).start()
-
-            @pl.when(me != z)
+                out_remote(what, p, z, near_h).start()
+
+    def send_far(what, p):
+        for z in [*range(half), *reversed(range(half, n))]:
+            other_side = jnp.logical_not(left) if z < half else left
+
+            @pl.when(other_side)
             def _():
                 out_remote(what, p, z, near_h).start()
 
@@ -324,8 +335,8 @@
             await_in(kind["k", p])
             await_in(kind["v", p])
             if p > 0:
-                send_out("g", p - 1)
-                send_out("l", p - 1)
+                send_far("g", p - 1)
+                send_far("l", p - 1)
             gacc[...] = jnp.zeros_like(gacc)
 
             def grad_step(z, carry):
@@ -365,7 +376,8 @@
 
             lax.fori_loop(0, n, update_step, 0)
             if p == periods - 1:
-                send_out("g", p)
+                send_far("g", p)
+            send_near("g", p)
             await_in(kind["q", p])
 
             def apply_step(z, carry):
@@ -394,7 +406,8 @@
 
             lax.fori_loop(0, n, apply_step, 0)
             if p == periods - 1:
-                send_out("l", p)
+                send_far("l", p)
+            send_near("l", p)
 
     def own_step(h):
         for i in range(3):

time: 172 us -> 173 us (level)
  no operation moved by 1% of the time
where the time goes in v3:
time: 173 us; the launch traced here: 172 us
  Pallas kernels  166 us (96%)
  local copies, waits for them, and re-layouts  5.5 us (3%)
    pallas_call x1, Pallas kernels, hub_shards(): pl.pallas_call(functools.partial(hub_kernel, n, periods), out_shape=(jax....  166 us
    unnamed x7, local copies, waits for them, and re-layouts  5.5 us

profile of v3, /device:TPU:9, one launch (start us, length us, event | category | flops | bytes accessed | tf_op | source)
XLA Modules:
  0.0 172.2 jit_solution(9221588912611045076)
XLA Ops:
  0.6 166.1 %shard_map.94 = (bf16[2,256,1024]{2,1,0:T(8,128)(2,1)}, f32[3,2,128,512]{3,2,1,0:T(8,128)}, f32[3,2,128,512]{3,2,1,0:T(8,128)}) custom-call(bf16[2,256,1024]{2,1,0:T(8,128)(2,1)} %q_ref.1, bf16[2,256,1024]{2,1,0:T(8,128)(2,1)} %k_ref.1, bf16[2,256,1024]{2,1,0:T(8,128)(2,1)} %v_ref.1, f32[2,2,256]{2,1,0:T(2,128)} %r_ref.1, f32[3,2,128,512]{3,2,1,0:T(8,128)} %w_ref.1, ...), custom_call_target="tpu_custom_call" | custom-call | tf_op jit(solution)/shard_map/pallas_call | solution.py:460
  166.7 0.0 copy-start.1
  166.7 2.4 %copy.13 = bf16[2,256,1024]{2,1,0:T(8,128)(2,1)} copy(bf16[2,256,1024]{2,1,0:T(8,128)(2,1)} %get-tuple-element.6) | data formatting | bytes 2097152
  169.1 0.0 copy-done.1
  169.1 0.0 copy-start
  169.1 1.1 copy.14
  170.3 0.8 copy-done
  171.1 1.1 copy.15
Async XLA Ops:
  166.7 2.4 %copy-start.1 = (f32[3,2,128,512]{3,2,1,0:T(8,128)S(1)}, f32[3,2,128,512]{3,2,1,0:T(8,128)}, u32[]{:S(2)}) copy-start(f32[3,2,128,512]{3,2,1,0:T(8,128)} %get-tuple-element.7) | copy-start | bytes 4718596
  169.1 2.0 %copy-start = (f32[3,2,128,512]{3,2,1,0:T(8,128)S(1)}, f32[3,2,128,512]{3,2,1,0:T(8,128)}, u32[]{:S(2)}) copy-start(f32[3,2,128,512]{3,2,1,0:T(8,128)} %get-tuple-element.8) | copy-start | bytes 4718596

commit v4 on v3

--- a/solution.py
+++ b/solution.py
@@ -241,20 +241,15 @@
         if i == kind["w"]:
             wb_ref[...] = w_ref[...].astype(jnp.bfloat16)
             mb_ref[...] = m_ref[...].astype(jnp.bfloat16)
+        in_remote(i, far_h, far_hub, 1, me).start()
 
         @pl.when(is_hub)
         def _():
             in_local(i).start()
-            in_remote(i, far_h, far_hub, 1, me).start()
 
         @pl.when(jnp.logical_not(is_hub))
         def _():
             in_remote(i, near_h, near_hub, 0, me).start()
-
-    @pl.when(jnp.logical_not(is_hub))
-    def _():
-        for i in range(len(inward)):
-            in_remote(i, far_h, far_hub, 1, me).start()
 
     def await_in(i):
         for z in range(n):

time: 173 us -> 172 us (level)
  no operation moved by 1% of the time
where the time goes in v4:
time: 172 us
  Pallas kernels  166 us (97%)
  local copies, waits for them, and re-layouts  5.5 us (3%)
    pallas_call x1, Pallas kernels, hub_shards(): pl.pallas_call(functools.partial(hub_kernel, n, periods), out_shape=(jax....  166 us
    unnamed x7, local copies, waits for them, and re-layouts  5.5 us

profile of v4, /device:TPU:9, one launch (start us, length us, event | category | flops | bytes accessed | tf_op | source)
XLA Modules:
  0.0 172.0 jit_solution(9494153893296046562)
XLA Ops:
  0.6 165.9 %shard_map.94 = (bf16[2,256,1024]{2,1,0:T(8,128)(2,1)}, f32[3,2,128,512]{3,2,1,0:T(8,128)}, f32[3,2,128,512]{3,2,1,0:T(8,128)}) custom-call(bf16[2,256,1024]{2,1,0:T(8,128)(2,1)} %q_ref.1, bf16[2,256,1024]{2,1,0:T(8,128)(2,1)} %k_ref.1, bf16[2,256,1024]{2,1,0:T(8,128)(2,1)} %v_ref.1, f32[2,2,256]{2,1,0:T(2,128)} %r_ref.1, f32[3,2,128,512]{3,2,1,0:T(8,128)} %w_ref.1, ...), custom_call_target="tpu_custom_call" | custom-call | tf_op jit(solution)/shard_map/pallas_call | solution.py:455
  166.5 0.0 copy-start.1
  166.5 2.4 %copy.13 = bf16[2,256,1024]{2,1,0:T(8,128)(2,1)} copy(bf16[2,256,1024]{2,1,0:T(8,128)(2,1)} %get-tuple-element.6) | data formatting | bytes 2097152
  168.9 0.0 copy-done.1
  168.9 0.0 copy-start
  168.9 1.1 copy.14
  170.1 0.8 copy-done
  170.9 1.1 copy.15
Async XLA Ops:
  166.5 2.4 %copy-start.1 = (f32[3,2,128,512]{3,2,1,0:T(8,128)S(1)}, f32[3,2,128,512]{3,2,1,0:T(8,128)}, u32[]{:S(2)}) copy-start(f32[3,2,128,512]{3,2,1,0:T(8,128)} %get-tuple-element.7) | copy-start | bytes 4718596
  168.9 2.0 %copy-start = (f32[3,2,128,512]{3,2,1,0:T(8,128)S(1)}, f32[3,2,128,512]{3,2,1,0:T(8,128)}, u32[]{:S(2)}) copy-start(f32[3,2,128,512]{3,2,1,0:T(8,128)} %get-tuple-element.8) | copy-start | bytes 4718596
